TPU v7x, 128 devices: a whole 4x4x4 slice. The times are simulated.
128 devices in a mesh: req: 16 (over z, y), mlp: 8 (over x, core).
Axes of the slice: x: 4, y: 4, z: 4, core: 2. Of those that a mesh axis runs over, the one named last changes fastest.
Arguments:
- activations: bfloat16 [8192, 4096], P('req', 'mlp')
- slot_segment: int32 [8192], P('req'), may hold values from -1 to 511, as said below
- attn_norm_gain: float32 [4096], replicated, may hold values from 0.5 to 1.5
- attn_norm_bias: float32 [4096], replicated, may hold values from -1.5 to 1.5
- mlp_norm_gain: float32 [4096], replicated, may hold values from 0.5 to 1.5
- mlp_norm_bias: float32 [4096], replicated, may hold values from -1.5 to 1.5
- qkv_weight: bfloat16 [4096, 6144], P(None, 'mlp')
- dense_weight: bfloat16 [2048, 4096], P('mlp'), may hold values from -0.1875 to 0.1875
- fc_weight: bfloat16 [4096, 8192], P(None, 'mlp'), may hold values from -0.09375 to 0.09375
- proj_weight: bfloat16 [8192, 4096], P('mlp'), may hold values from -0.09375 to 0.09375
Outputs:
- output_rows: float32 [8192, 4096], P('req', 'mlp')
- cache_rows: bfloat16 [2, 4096, 2048], P(None, 'req', 'mlp')
Inputs may be any that keep to these rules, and one draw needn't show every extreme that they name: `slot_segment`: each group's 512 slots hold live slots first and -1 after them; the live count of every group is a multiple of 16 between 16 and 512, the counts of all groups sum to 4096, and some group is full, its last slot beginning a prompt of one token. A live slot holds the group slot where its prompt begins; a prompt's slots are consecutive.
All inputs are finite; a program needn't handle non-finite values.
Results may differ from a plain program's by a relative error of at most 0.0047.
The roundings to bfloat16 on the way count: a program that leaves them out, or rounds other values in their place, can miss the bound.
Values may be sent and summed in bfloat16 or wider, within the bound.
A program may use at most 128 MiB of HBM per device.

v0:
```python
import jax
import jax.numpy as jnp
from jax import lax
from jax.sharding import PartitionSpec as P

HD = 128
ROT = 32
LIVE_DEV = 256


def layer_norm(row_data, gain_vec, bias_vec):
    row_data = row_data.astype(jnp.float32)
    row_mean = jnp.mean(row_data, axis=-1, keepdims=True)
    centered = row_data - row_mean
    variance = jnp.mean(centered * centered, axis=-1, keepdims=True)
    return (centered * lax.rsqrt(variance + 1e-05) * gain_vec + bias_vec).astype(jnp.bfloat16)


def rotate(head_data, position):
    half_rot = ROT // 2
    inv_freq = 10000.0 ** (-(jnp.arange(half_rot).astype(jnp.float32) * 2.0 / ROT))
    angles = position.astype(jnp.float32)[:, None] * inv_freq[None, :]
    cosine = jnp.concatenate([jnp.cos(angles), jnp.cos(angles)], axis=-1)[:, None, :]
    sine_part = jnp.concatenate([jnp.sin(angles), jnp.sin(angles)], axis=-1)[:, None, :]
    rot_part = head_data[..., :ROT]
    pass_part = head_data[..., ROT:]
    first_half = rot_part[..., :half_rot]
    second = rot_part[..., half_rot:]
    turned = jnp.concatenate([-second, first_half], axis=-1)
    return jnp.concatenate([rot_part * cosine + turned * sine_part, pass_part], axis=-1)


def attend(normed, segment, qkv_weight):
    slot_count = normed.shape[0]
    head_count = qkv_weight.shape[1] // (3 * HD)
    mixed_proj = jnp.dot(normed, qkv_weight, preferred_element_type=jnp.float32).reshape(
        slot_count, head_count, 3, HD
    )
    slot_index = jnp.arange(slot_count, dtype=jnp.int32)
    position = slot_index - segment
    query_rows = rotate(mixed_proj[:, :, 0], position).astype(jnp.bfloat16)
    key_rows = rotate(mixed_proj[:, :, 1], position).astype(jnp.bfloat16)
    value_rows = mixed_proj[:, :, 2].astype(jnp.bfloat16)
    scores = jnp.einsum(
        "qhd,khd->hqk", query_rows, key_rows, preferred_element_type=jnp.float32
    ) * HD ** (-0.5)
    allowed = (
        (segment[:, None] == segment[None, :])
        & (slot_index[None, :] <= slot_index[:, None])
        & (segment[:, None] >= 0)
    )
    scores = jnp.where(allowed[None], scores, -1e30)
    row_max = jnp.max(scores, axis=-1, keepdims=True)
    weights = jnp.exp(scores - row_max)
    prob_rows = (weights / jnp.sum(weights, axis=-1, keepdims=True)).astype(jnp.bfloat16)
    context = jnp.einsum("hqk,khd->qhd", prob_rows, value_rows, preferred_element_type=jnp.float32)
    context = context.astype(jnp.bfloat16).reshape(slot_count, head_count * HD)
    return (
        context,
        key_rows.reshape(slot_count, head_count * HD),
        value_rows.reshape(slot_count, head_count * HD),
    )


def body(
    activations,
    slot_segment,
    attn_norm_gain,
    attn_norm_bias,
    mlp_norm_gain,
    mlp_norm_bias,
    qkv_weight,
    dense_weight,
    fc_weight,
    proj_weight,
):
    slot_count = activations.shape[0]
    groups = lax.axis_size("req")
    per_peer = slot_count // groups
    live_slot = slot_segment >= 0
    group_fill = lax.all_gather(
        jnp.sum(live_slot.astype(jnp.int32)).reshape(1), "req", axis=0, tiled=True
    )
    group_units = group_fill // groups
    received_live = (jnp.arange(per_peer, dtype=jnp.int32)[None, :] < group_units[:, None]).reshape(
        -1
    )
    live_rank = jnp.cumsum(received_live.astype(jnp.int32)) - 1
    target = jnp.where(received_live, live_rank, LIVE_DEV)
    pick_rows = (
        jnp.zeros((LIVE_DEV,), jnp.int32)
        .at[target]
        .set(jnp.arange(groups * per_peer, dtype=jnp.int32), mode="drop")
    )
    full_rows = lax.all_gather(activations, "mlp", axis=1, tiled=True)
    normed = layer_norm(full_rows, attn_norm_gain, attn_norm_bias)
    context, key_rows, value_rows = attend(normed, slot_segment, qkv_weight)
    key_value = jnp.concatenate([key_rows, value_rows], axis=1).reshape(per_peer, groups, -1)
    cache_rows = lax.all_to_all(key_value, "req", split_axis=1, concat_axis=0, tiled=True)
    cache_rows = jnp.take(cache_rows.reshape(groups * per_peer, -1), pick_rows, axis=0)
    width = key_rows.shape[1]
    cache_rows = jnp.stack([cache_rows[:, :width], cache_rows[:, width:]])
    mlp_normed = layer_norm(full_rows, mlp_norm_gain, mlp_norm_bias)
    hidden = jax.nn.gelu(
        jnp.dot(mlp_normed, fc_weight, preferred_element_type=jnp.float32), approximate=False
    )
    hidden = hidden.astype(jnp.bfloat16)
    part = jnp.dot(context, dense_weight, preferred_element_type=jnp.float32) + jnp.dot(
        hidden, proj_weight, preferred_element_type=jnp.float32
    )
    total = lax.psum_scatter(
        part.astype(jnp.bfloat16), "mlp", scatter_dimension=1, tiled=True
    ).astype(jnp.float32)
    combined = activations.astype(jnp.float32) + total
    output_rows = jnp.where(live_slot[:, None], combined, 0.0)
    return (output_rows, cache_rows)


def solution(mesh):
    placed = (
        P("req", "mlp"),
        P("req"),
        P(),
        P(),
        P(),
        P(),
        P(None, "mlp"),
        P("mlp", None),
        P(None, "mlp"),
        P("mlp", None),
    )
    return jax.shard_map(
        body,
        mesh=mesh,
        in_specs=placed,
        out_specs=(P("req", "mlp"), P(None, "req", "mlp")),
        check_vma=False,
    )
```

profile of v0, /device:TPU:0, one launch (start us, length us, event | category | flops | bytes accessed | tf_op | source)
XLA Modules:
  0.0 147.7 jit_solution(17991416886373539449)
XLA Ops:
  8.0 1.3 convert_reduce_fusion.1
  10.5 1.0 fusion.71
  11.5 1.0 copy.46
  12.6 31.7 %all-gather.2.cloned.1.call-done = bf16[512,4096]{1,0:T(8,128)(2,1)} async-done(((bf16[512,512]{1,0:T(8,128)(2,1)}), bf16[512,4096]{1,0:T(8,128)(2,1)}) %all-gather.2.cloned.1.call-update) | async-done | bytes 4194320 | tf_op jit(solution)/shard_map/all_gather | solution.py:95
  44.3 3.0 %convert_reduce_fusion = f32[512]{0:T(512)S(1)} fusion(bf16[512,4096]{1,0:T(8,128)(2,1)} %all-gather.2.cloned.1.call-done), kind=kLoop, calls=%fused_computation.4 | loop fusion | flops 4193792 | bytes 4196352 | tf_op jit(solution)/shard_map/reduce_sum | solution.py:13
  47.7 1.2 fusion.9
  49.0 6.6 %fusion.12 = f32[512,768]{0,1:T(8,128)S(1)} fusion(bf16[4096,768]{1,0:T(8,128)(2,1)} %param.16, bf16[512,4096]{1,0:T(8,128)(2,1)S(1)} %copy-done.1, f32[4096]{0:T(1024)S(1)} %copy-done.10, f32[4096]{0:T(1024)S(1)} %copy-done.11, f32[512]{0:T(512)S(1)} %add_rsqrt_fusion, f32[512]{0:T(512)S(1)} %broadcast_multiply_fusion), kind=kOutput, calls=%fused_computation.16 | convolution fusion | flops 3233808384 | bytes 12095488 | tf_op jit(solution)/shard_map/dot_general | solution.py:36
  56.3 0.9 fusion.137
  57.4 0.9 slice.78
  58.2 1.1 slice_negate_fusion
  59.4 1.2 copy.58
  60.7 0.8 slice.98
  63.6 2.1 %fusion.138 = f32[2,512]{1,0:T(2,128)S(1)} fusion(pred[512,512]{0,1:T(8,128)(4,1)} %copy.46, bf16[512,2,128]{2,0,1:T(8,128)(2,1)S(1)} %maximum_convert_fusion, bf16[512,2,96]{2,0,1:T(8,128)(2,1)} %slice.98, bf16[512,2,32]{2,0,1:T(8,128)(2,1)S(1)} %fusion.75), kind=kOutput, calls=%fused_computation.173 | convolution fusion | flops 136839680 | bytes 790528 | tf_op jit(solution)/shard_map/sub | solution.py:54
  65.8 2.3 %convolution_convert_fusion = bf16[2,128,512]{2,1,0:T(8,128)(2,1)S(1)} fusion(f32[2,512]{1,0:T(2,128)S(1)} %fusion.138, bf16[512,2,1,128]{0,3,1,2:T(8,128)(2,1)S(1)} %copy-done.7, pred[512,512]{0,1:T(8,128)(4,1)} %copy.46, bf16[512,2,128]{2,0,1:T(8,128)(2,1)S(1)} %maximum_convert_fusion, bf16[512,2,96]{2,0,1:T(8,128)(2,1)S(1)} %copy-done.9, ...), kind=kOutput, calls=%fused_computation.49 | convolution fusion | flops 271713792 | bytes 1314816 | tf_op jit(solution)/shard_map/hqk,khd->qhd/dot_general | solution.py:56
  68.1 23.6 %fusion.35 = f32[512,4096]{1,0:T(8,128)} fusion(bf16[1024,4096]{1,0:T(8,128)(2,1)} %param.19, bf16[4096,1024]{1,0:T(8,128)(2,1)} %param.18, bf16[512,4096]{1,0:T(8,128)(2,1)} %all-gather.2.cloned.1.call-done, f32[4096]{0:T(1024)S(1)} %copy-done.12, f32[4096]{0:T(1024)S(1)} %copy-done.13, f32[512]{0:T(512)S(1)} %add_rsqrt_fusion, ...), kind=kOutput, calls=%fused_computation.47 | convolution fusion | flops 8636596224 | bytes 29396992 | tf_op jit(solution)/shard_map/dot_general | solution.py:108
  91.7 6.6 %add_convert_fusion = bf16[512,4096]{1,0:T(8,128)(2,1)} fusion(f32[512,4096]{1,0:T(8,128)} %fusion.35, bf16[512,256]{0,1:T(8,128)(2,1)S(1)} %bitcast.45, bf16[256,4096]{1,0:T(8,128)(2,1)S(1)} %copy-done), kind=kOutput, calls=%fused_computation.14 | convolution fusion | flops 1077936128 | bytes 14942208 | tf_op jit(solution)/shard_map/dot_general | solution.py:108
  99.6 1.4 dynamic-update-slice
  101.0 16.5 %all-reduce = s32[16]{0:T(128)S(1)} all-reduce(s32[16]{0:T(128)S(1)} %dynamic-update-slice), channel_id=1, replica_groups=mesh['req'=16,'mlp'=8] {'req'}, use_global_device_ids=true, to_apply=%add | all-reduce | flops 16 | bytes 128
  118.6 2.4 %scatter_custom_fusion = s32[256]{0:T(256)S(1)} fusion(s32[512]{0:T(512)S(1)} %bitcast.47, s32[512]{0:T(512)S(1)} %iota.32, s32[]{:T(128)} %constant.46.clone.1), kind=kCustom, calls=%fused_computation.131 | custom fusion | bytes 1028 | tf_op jit(solution)/shard_map/scatter | solution.py:93
  121.9 1.1 copy.54
  123.0 3.6 %all-to-all-start = ((bf16[32,16,512]{2,0,1:T(8,128)(2,1)}), bf16[32,16,512]{2,0,1:T(8,128)(2,1)S(1)}, u32[]{:S(2)}, u32[]{:S(2)}) async-start(bf16[32,16,512]{2,0,1:T(8,128)(2,1)} %copy.54), calls=%async_computation.1 | async-start | bytes 1048576 | tf_op jit(solution)/shard_map/all_to_all | solution.py:99
  126.6 10.1 %all-to-all-done = bf16[32,16,512]{2,0,1:T(8,128)(2,1)S(1)} async-done(((bf16[32,16,512]{2,0,1:T(8,128)(2,1)}), bf16[32,16,512]{2,0,1:T(8,128)(2,1)S(1)}, u32[]{:S(2)}, u32[]{:S(2)}) %all-to-all-start) | async-done | bytes 524320 | tf_op jit(solution)/shard_map/all_to_all | solution.py:99
  136.7 1.2 gather_fusion
  138.7 2.2 %add_select_fusion = f32[512,512]{1,0:T(8,128)} fusion(bf16[512,512]{1,0:T(8,128)(2,1)} %reduce-scatter.2.cloned.1.call-done, bf16[512,512]{1,0:T(8,128)(2,1)S(1)} %copy-done.3, pred[512]{0:T(512)(128)(4,1)S(1)} %get-tuple-element.3), kind=kLoop, calls=%fused_computation.50 | loop fusion | flops 1048576 | bytes 2097664 | tf_op jit(solution)/shard_map/jit(_where)/select_n | solution.py:115
  (77 shorter events, 9.5 us)
Async XLA Ops:
  7.2 84.6 %copy-start = (bf16[256,4096]{1,0:T(8,128)(2,1)S(1)}, bf16[256,4096]{1,0:T(8,128)(2,1)}, u32[]{:S(2)}) copy-start(bf16[256,4096]{1,0:T(8,128)(2,1)} %param.17) | copy-start | bytes 6291460
  7.2 37.1 %all-gather.2.cloned.1.call-start = ((), (), s32[]{:S(2)}) async-start(), calls=%async_computation.2 | async-start | bytes 4718592 | tf_op jit(solution)/shard_map/all_gather | solution.py:95
  7.9 130.8 %reduce-scatter.2.cloned.1.call-start = ((), (), s32[]{:S(2)}) async-start(), calls=%async_computation.3 | async-start | bytes 4718592 | tf_op jit(solution)/shard_map/reduce_scatter | solution.py:111
  44.3 3.4 %copy-start.1 = (bf16[512,4096]{1,0:T(8,128)(2,1)S(1)}, bf16[512,4096]{1,0:T(8,128)(2,1)}, u32[]{:S(2)}) copy-start(bf16[512,4096]{1,0:T(8,128)(2,1)} %all-gather.2.cloned.1.call-done) | copy-start | bytes 12582916
  47.7 1.2 copy-start.10
  47.7 1.2 copy-start.11
  60.6 1.1 copy-start.2
  60.6 1.2 copy-start.4
  60.7 1.4 copy-start.5
  61.5 1.0 copy-start.6
  62.9 0.7 copy-start.8
  63.6 2.1 %copy-start.7 = (bf16[512,2,1,128]{0,3,1,2:T(8,128)(2,1)S(1)}, bf16[512,2,1,128]{0,3,1,2:T(8,128)(2,1)}, u32[]{:S(2)}) copy-start(bf16[512,2,1,128]{0,3,1,2:T(8,128)(2,1)} %fusion.76) | copy-start | bytes 786436
  63.6 2.1 %copy-start.9 = (bf16[512,2,96]{2,0,1:T(8,128)(2,1)S(1)}, bf16[512,2,96]{2,0,1:T(8,128)(2,1)}, u32[]{:S(2)}) copy-start(bf16[512,2,96]{2,0,1:T(8,128)(2,1)} %slice.98) | copy-start | bytes 589828
  65.7 2.3 %copy-start.12 = (f32[4096]{0:T(1024)S(1)}, f32[4096]{0:T(1024)}, u32[]{:S(2)}) copy-start(f32[4096]{0:T(1024)} %param.15) | copy-start | bytes 49156
  65.8 2.3 %copy-start.13 = (f32[4096]{0:T(1024)S(1)}, f32[4096]{0:T(1024)}, u32[]{:S(2)}) copy-start(f32[4096]{0:T(1024)} %param.14) | copy-start | bytes 49156
  98.4 0.7 copy-start.14
  123.0 13.7 %all-to-all-start = ((bf16[32,16,512]{2,0,1:T(8,128)(2,1)}), bf16[32,16,512]{2,0,1:T(8,128)(2,1)S(1)}, u32[]{:S(2)}, u32[]{:S(2)}) async-start(bf16[32,16,512]{2,0,1:T(8,128)(2,1)} %copy.54), calls=%async_computation.1 | async-start | bytes 1048576 | tf_op jit(solution)/shard_map/all_to_all | solution.py:99
  126.6 12.1 %copy-start.3 = (bf16[512,512]{1,0:T(8,128)(2,1)S(1)}, bf16[512,512]{1,0:T(8,128)(2,1)}, u32[]{:S(2)}) copy-start(bf16[512,512]{1,0:T(8,128)(2,1)} %param.10) | copy-start | bytes 1572868
Sparse Core Ops, SparseCore 0:
  9.7 34.5 all-gather.1
  98.5 38.3 reduce-scatter.1
where the time goes:
time: 148 us
  waiting for transfers between devices  42.5 us (29%)
  matrix products  41.2 us (28%)
  local copies, waits for them, and re-layouts  17.2 us (12%)
  blocking collectives  16.5 us (11%)
  between operations  14.4 us (10%)
  other arithmetic  12.3 us (8%)
  starting transfers between devices  3.65 us (2%)
    all_gather x1, waiting for transfers between devices, body(): full_rows = lax.all_gather(activations, 'mlp', axis=1, tiled=True)  31.7 us
    dot_general x1, matrix products, body(): jnp.dot(hidden, proj_weight, preferred_element_type=jnp.float32)  23.6 us
    unnamed x1, blocking collectives  16.5 us
    all_to_all x1, waiting for transfers between devices, body(): lax.all_to_all(key_value, 'req', split_axis=1, concat_axis=0, tiled=True)  10.1 us
    dot_general x1, matrix products, body(): jnp.dot(context, dense_weight, preferred_element_type=jnp.float32)  6.64 us
    dot_general x1, matrix products, attend(): jnp.dot(normed, qkv_weight, preferred_element_type=jnp.float32)  6.56 us
    unnamed x35, local copies, waits for them, and re-layouts  5.81 us
    all_to_all x1, starting transfers between devices, body(): lax.all_to_all(key_value, 'req', split_axis=1, concat_axis=0, tiled=True)  3.57 us
  transfers between devices with their start and end apart: 3, of which 2 were waited for; matrix products, arithmetic and copies ran while one was open for 9% of the time, Pallas kernels for 0%

commit v1 on v0

v1 whole, which is shorter than its diff:
```python
import functools
import math

import jax
import jax.numpy as jnp
from jax import lax
from jax.experimental import pallas as pl
from jax.experimental.pallas import tpu as pltpu
from jax.sharding import PartitionSpec as P

HD = 128
ROT = 32
F32 = jnp.float32
BF16 = jnp.bfloat16
MESH = pl.DeviceIdType.MESH

LA, LB, OA, RA, RB, OB, PP, PL, PR, POA, POB = range(11)
OWN, RIGHT, OPP, LEFT = 0, 1, 2, 3


def remote(src, dst, send_sem, recv_sem, dev):
    return pltpu.make_async_remote_copy(
        src_ref=src,
        dst_ref=dst,
        send_sem=send_sem,
        recv_sem=recv_sem,
        device_id=dev,
        device_id_type=MESH,
    )


def layer_kernel(
    groups,
    members,
    act,
    seg,
    g1,
    b1,
    g2,
    b2,
    wq_h,
    wd_h,
    wf_h,
    wp_h,
    out,
    cache,
    xf,
    wq,
    wf,
    wo,
    n1,
    n2,
    gs,
    segc,
    tab,
    qb,
    kvb,
    hc,
    kvp,
    kvr,
    cnt_s,
    cnt_r,
    psend,
    precv,
    mine,
    lo_s,
    lo_r,
    lb_s,
    lb_r,
    wsem,
    lsem,
    ag_ss,
    ag_rs,
    kv_ss,
    kv_rs,
    ct_ss,
    ct_rs,
    p_ss,
    p_rs,
    lo_ss,
    lo_rs,
    lb_ss,
    lb_rs,
):
    rows = xf.shape[2]
    half = rows // 2
    width = xf.shape[3]
    chips = members // 2
    model = members * width
    heads = qb.shape[1] // HD
    kv_w = heads * HD
    per_peer = kvp.shape[0] // groups
    me_g = lax.axis_index("req")
    me = lax.axis_index("mlp")
    core = lax.rem(me, 2)
    chip = me // 2
    right = lax.rem(me + 2, members)
    left = lax.rem(me + members - 2, members)
    opp = lax.rem(me + members // 2, members)
    flip = 1 - 2 * core
    partner = me + flip
    to_right, to_left, to_partner = (me_g, right), (me_g, left), (me_g, partner)

    copies = [
        pltpu.make_async_copy(wq_h, wq, wsem.at[0]),
        pltpu.make_async_copy(wf_h, wf, wsem.at[1]),
        pltpu.make_async_copy(wd_h, wo.at[pl.ds(0, kv_w)], wsem.at[2]),
        pltpu.make_async_copy(wp_h, wo.at[pl.ds(kv_w, wo.shape[0] - kv_w)], wsem.at[3]),
    ]
    own_copies = [
        pltpu.make_async_copy(act.at[pl.ds(h * rows, rows)], xf.at[h, me], lsem.at[h])
        for h in range(2)
    ]

    barrier = pltpu.get_barrier_semaphore()
    for dev in (to_right, to_left, to_partner):
        pl.semaphore_signal(barrier, inc=1, device_id=dev, device_id_type=MESH)

    def greet(t, carry):
        peer = lax.rem(me_g + t, groups)
        pl.semaphore_signal(barrier, inc=1, device_id=(peer, me), device_id_type=MESH)
        return carry

    lax.fori_loop(1, groups, greet, 0)
    for c in own_copies + copies:
        c.start()
    pl.semaphore_wait(barrier, 3 + groups - 1)

    lo_rows, hi_rows = pl.ds(0, half), pl.ds(half, half)

    def ag(h, kind, src, dst, dev):
        return remote(src, dst, ag_ss.at[h, kind], ag_rs.at[h, kind], dev)

    def got(h, kind, ref):
        remote(ref, ref, ag_ss.at[h, kind], ag_rs.at[h, kind], to_partner).wait_recv()

    sent = []

    def go(copy):
        copy.start()
        sent.append(copy)

    def gather_own(h):
        a = act.at[pl.ds(h * rows, half)]
        b = act.at[pl.ds(h * rows + half, half)]
        go(ag(h, LA, a, xf.at[h, me, lo_rows], to_right))
        go(ag(h, RB, b, xf.at[h, me, hi_rows], to_left))
        go(ag(h, LB, b, xf.at[h, me, hi_rows], to_right))
        go(ag(h, RA, a, xf.at[h, me, lo_rows], to_left))
        go(ag(h, PP, act.at[pl.ds(h * rows, rows)], xf.at[h, me], to_partner))

    def gather_far(h):
        got(h, LA, xf.at[h, left, lo_rows])
        go(ag(h, OA, xf.at[h, left, lo_rows], xf.at[h, left, lo_rows], to_right))
        got(h, RB, xf.at[h, right, hi_rows])
        go(ag(h, OB, xf.at[h, right, hi_rows], xf.at[h, right, hi_rows], to_left))

    def gather_near(h):
        got(h, LB, xf.at[h, left, hi_rows])
        go(ag(h, PL, xf.at[h, left], xf.at[h, left], to_partner))
        got(h, RA, xf.at[h, right, lo_rows])
        go(ag(h, PR, xf.at[h, right], xf.at[h, right], to_partner))

    def gather_opp(h):
        got(h, OA, xf.at[h, opp, lo_rows])
        go(ag(h, POA, xf.at[h, opp, lo_rows], xf.at[h, opp, lo_rows], to_partner))
        got(h, OB, xf.at[h, opp, hi_rows])
        go(ag(h, POB, xf.at[h, opp, hi_rows], xf.at[h, opp, hi_rows], to_partner))

    def gather_end(h):
        own_copies[h].wait()
        got(h, PP, xf.at[h, partner])
        got(h, PL, xf.at[h, left + flip])
        got(h, PR, xf.at[h, right + flip])
        got(h, POA, xf.at[h, opp + flip, lo_rows])
        got(h, POB, xf.at[h, opp + flip, hi_rows])

    gather_own(0)

    for i, ref in enumerate((g1, b1, g2, b2)):
        for m in range(members):
            for t in range(width // 128):
                k = m * (width // 128) + t
                gs[i, m : m + 1, t * 128 : (t + 1) * 128] = ref[k : k + 1, :]
    live_sum = jnp.sum((seg[...] >= 0).astype(F32), axis=1, keepdims=True)
    units = jnp.sum(live_sum, axis=0, keepdims=True) * (1.0 / groups)
    cnt_s[...] = jnp.broadcast_to(units, cnt_s.shape)
    for b in range(seg.shape[0]):
        block = jnp.broadcast_to(seg[b : b + 1, :].astype(F32), (128, 128))
        segc[b * 128 : (b + 1) * 128, :] = block.T

    lane = lax.broadcasted_iota(jnp.int32, (128, 128), 1)
    pair = lax.rem(lane, ROT // 2).astype(F32)
    freq = jnp.where(lane < ROT, jnp.exp(pair * (-2.0 / ROT * math.log(10000.0))), 0.0)

    def angles(b, carry):
        at = pl.ds(pl.multiple_of(b * 128, 128), 128)
        slot = (b * 128 + lax.broadcasted_iota(jnp.int32, (128, 128), 0)).astype(F32)
        ang = (slot - segc[at, :]) * freq
        sine = jnp.sin(ang)
        tab[0, at, :] = jnp.cos(ang)
        tab[1, at, :] = jnp.where(lane < ROT // 2, -sine, 0.0)
        tab[2, at, :] = jnp.where(lane < ROT // 2, 0.0, sine)
        return carry

    gather_far(0)
    gather_own(1)
    lax.fori_loop(0, seg.shape[0], angles, 0)
    gather_near(0)
    gather_opp(0)

    def count_out(t, carry):
        peer = lax.rem(me_g + t, groups)
        remote(cnt_s, cnt_r.at[me_g], ct_ss.at[t], ct_rs.at[t], (peer, me)).start()
        return carry

    lax.fori_loop(1, groups, count_out, 0)

    def norms(h):
        def body(r, carry):
            at = pl.ds(pl.multiple_of(r * 16, 16), 16)
            xs = [xf[h, m, at, :].astype(F32) for m in range(members)]
            total = functools.reduce(lambda a, b: a + b, xs)
            mean = jnp.sum(total, axis=-1, keepdims=True) * (1.0 / model)
            cs = [x - mean for x in xs]
            square = functools.reduce(lambda a, b: a + b, [c * c for c in cs])
            scale = lax.rsqrt(jnp.sum(square, axis=-1, keepdims=True) * (1.0 / model) + 1e-05)
            for m in range(members):
                y = cs[m] * scale
                cols = slice(m * width, (m + 1) * width)
                n1[at, cols] = (y * gs[0, m : m + 1, :] + gs[1, m : m + 1, :]).astype(BF16)
                n2[at, cols] = (y * gs[2, m : m + 1, :] + gs[3, m : m + 1, :]).astype(BF16)
            return carry

        lax.fori_loop(0, rows // 16, body, 0)

    def project(h):
        at = slice(h * rows, (h + 1) * rows)
        parts = []
        for n in range(wq.shape[1] // 256):
            acc = jnp.dot(n1[...], wq[:, n * 256 : (n + 1) * 256], preferred_element_type=F32)
            parts += [acc[:, :HD], acc[:, HD:]]
        cos, s1, s2 = tab[0, at, :], tab[1, at, :], tab[2, at, :]

        def turn(u):
            return u * cos + pltpu.roll(u, HD - ROT // 2, 1) * s1 + pltpu.roll(u, ROT // 2, 1) * s2

        for i in range(heads):
            cols = slice(i * HD, (i + 1) * HD)
            qb[:, cols] = turn(parts[3 * i]).astype(BF16)
            kvb[at, cols] = turn(parts[3 * i + 1]).astype(BF16)
            kvb[at, kv_w + i * HD : kv_w + (i + 1) * HD] = parts[3 * i + 2].astype(BF16)

    def attend(h):
        keys = (h + 1) * rows
        first = jnp.concatenate([segc[h * rows : (h + 1) * rows, :]] * (keys // 128), axis=1)
        query = (h * rows + lax.broadcasted_iota(jnp.int32, (rows, keys), 0)).astype(F32)
        key = lax.broadcasted_iota(jnp.int32, (rows, keys), 1).astype(F32)
        allowed = (key >= first) & (key <= query)
        for i in range(heads):
            cols = slice(i * HD, (i + 1) * HD)
            s = lax.dot_general(
                qb[:, cols],
                kvb[0:keys, cols],
                (((1,), (1,)), ((), ())),
                preferred_element_type=F32,
            ) * (HD**-0.5)
            s = jnp.where(allowed, s, -1e30)
            w = jnp.exp(s - jnp.max(s, axis=-1, keepdims=True))
            p = (w / jnp.sum(w, axis=-1, keepdims=True)).astype(BF16)
            ctx = jnp.dot(
                p, kvb[0:keys, kv_w + i * HD : kv_w + (i + 1) * HD], preferred_element_type=F32
            )
            hc[:, cols] = ctx.astype(BF16)

    def expand(h):
        for n in range(wf.shape[1] // 256):
            cols = slice(n * 256, (n + 1) * 256)
            u = jnp.dot(n2[...], wf[:, cols], preferred_element_type=F32)
            u = 0.5 * u * (1.0 + lax.erf(u * (0.5**0.5)))
            hc[:, kv_w + n * 256 : kv_w + (n + 1) * 256] = u.astype(BF16)

    def pcopy(h, rel):
        return remote(psend.at[h, rel], precv.at[h, rel], p_ss.at[h, rel], p_rs.at[h, rel], to_partner)

    def contract(h, rel):
        block = 2 * lax.rem(chip + rel, chips)
        for theirs in (True, False):
            col = (block + (1 - core if theirs else core)) * width
            acc = jnp.dot(
                hc[...],
                wo[:, pl.ds(pl.multiple_of(col, width), width)],
                preferred_element_type=F32,
            )
            if theirs:
                psend[h, rel] = acc.astype(BF16)
                go(pcopy(h, rel))
            else:
                mine[h, rel] = acc

    def chip_sum(h, rel, at=slice(None)):
        return mine[h, rel, at, :] + precv[h, rel, at, :].astype(F32)

    def low(h, way):
        dev = to_right if way == 0 else to_left
        return remote(lo_s.at[h, way], lo_r.at[h, way], lo_ss.at[h, way], lo_rs.at[h, way], dev)

    def back(h, way, piece):
        dev = to_right if way == 0 else to_left
        return remote(
            lb_s.at[h, way, piece],
            lb_r.at[h, way, piece],
            lb_ss.at[h, way, piece],
            lb_rs.at[h, way, piece],
            dev,
        )

    top, bottom = slice(0, half), slice(half, rows)

    def scatter_opp(h):
        pcopy(h, OPP).wait_recv()
        lo_s[h, 0] = chip_sum(h, OPP, top).astype(BF16)
        go(low(h, 0))
        lo_s[h, 1] = chip_sum(h, OPP, bottom).astype(BF16)
        go(low(h, 1))

    def scatter_near(h, way):
        rel = RIGHT if way == 0 else LEFT
        piece = 1 - way
        pcopy(h, rel).wait_recv()
        lb_s[h, way, piece] = chip_sum(h, rel, (top, bottom)[piece]).astype(BF16)
        go(back(h, way, piece))

    def scatter_far(h):
        for way in range(2):
            rel = RIGHT if way == 0 else LEFT
            piece = way
            low(h, way).wait_recv()
            total = chip_sum(h, rel, (top, bottom)[piece]) + lo_r[h, way].astype(F32)
            lb_s[h, way, piece] = total.astype(BF16)
            go(back(h, way, piece))

    def finish(h):
        pcopy(h, OWN).wait_recv()
        for piece in range(2):
            for way in range(2):
                back(h, way, piece).wait_recv()
            at = (top, bottom)[piece]
            total = chip_sum(h, OWN, at)
            total = total + lb_r[h, 0, piece].astype(F32) + lb_r[h, 1, piece].astype(F32)
            base = h * rows + piece * half
            x = xf[h, me, at, :].astype(F32)
            first = jnp.concatenate([segc[base : base + half, :]] * (width // 128), axis=1)
            out[base : base + half, :] = jnp.where(first >= 0.0, x + total, 0.0)

    def cache_out():
        slots = kvp.shape[0]
        r = lax.broadcasted_iota(jnp.int32, (slots, slots), 0)
        s = lax.broadcasted_iota(jnp.int32, (slots, slots), 1)
        pick = s == lax.rem(r, per_peer) * groups + r // per_peer
        pick = jnp.where(pick, 1.0, 0.0).astype(BF16)
        kvp[...] = jnp.dot(pick, kvb[...], preferred_element_type=F32).astype(BF16)

        def body(t, carry):
            peer = lax.rem(me_g + t, groups)
            kv_copy(t, peer).start()
            return carry

        lax.fori_loop(1, groups, body, 0)

    def kv_copy(t, peer):
        src = kvp.at[pl.ds(pl.multiple_of(peer * per_peer, per_peer), per_peer)]
        dst = kvr.at[pl.ds(pl.multiple_of(me_g * per_peer, per_peer), per_peer)]
        return remote(src, dst, kv_ss.at[t], kv_rs.at[t], (peer, me))

    def cache_in():
        here = pl.ds(pl.multiple_of(me_g * per_peer, per_peer), per_peer)
        kvr[here, :] = kvp[here, :]
        cnt_r[me_g] = cnt_s[...]

        def body(t, carry):
            peer = lax.rem(me_g + groups - t, groups)
            from_peer = pl.ds(pl.multiple_of(peer * per_peer, per_peer), per_peer)
            dst = kvr.at[from_peer]
            remote(dst, dst, kv_ss.at[t], kv_rs.at[t], (peer, me)).wait_recv()
            dst = cnt_r.at[peer]
            remote(dst, dst, ct_ss.at[t], ct_rs.at[t], (peer, me)).wait_recv()
            return carry

        lax.fori_loop(1, groups, body, 0)
        per_block = 128 // per_peer
        live_rows = cache.shape[1]
        row = lax.broadcasted_iota(jnp.int32, (live_rows, 128), 0).astype(F32)
        lane1 = lax.broadcasted_iota(jnp.int32, (1, 128), 1)
        owner = lane1 // per_peer
        unit = lax.rem(lane1, per_peer).astype(F32)
        before = jnp.zeros((1, 128), F32)
        acc = jnp.zeros((live_rows, kvr.shape[1]), F32)
        for b in range(groups // per_block):
            have = jnp.zeros((1, 128), F32)
            start = jnp.zeros((1, 128), F32)
            for t in range(per_block):
                count = cnt_r[b * per_block + t, 0:1, :]
                have = jnp.where(owner == t, count, have)
                start = jnp.where(owner == t, before, start)
                before = before + count
            place = jnp.where(unit < have, start + unit, -1.0)
            pick = jnp.where(row == place, 1.0, 0.0).astype(BF16)
            acc = acc + jnp.dot(
                pick, kvr[b * 128 : (b + 1) * 128, :], preferred_element_type=F32
            )
        cache[0] = acc[:, :kv_w].astype(BF16)
        cache[1] = acc[:, kv_w:].astype(BF16)

    gather_end(0)
    norms(0)
    copies[0].wait()
    project(0)
    gather_far(1)
    attend(0)
    copies[1].wait()
    expand(0)
    gather_near(1)
    copies[2].wait()
    copies[3].wait()
    contract(0, OPP)
    contract(0, RIGHT)
    gather_opp(1)
    scatter_opp(0)
    contract(0, LEFT)
    scatter_near(0, 0)
    contract(0, OWN)
    scatter_near(0, 1)
    gather_end(1)
    norms(1)
    scatter_far(0)
    project(1)
    cache_out()
    attend(1)
    expand(1)
    contract(1, OPP)
    contract(1, RIGHT)
    scatter_opp(1)
    contract(1, LEFT)
    scatter_near(1, 0)
    contract(1, OWN)
    scatter_near(1, 1)
    finish(0)
    cache_in()
    scatter_far(1)
    finish(1)

    for copy in sent:
        copy.wait_send()

    def drain(t, carry):
        peer = lax.rem(me_g + t, groups)
        kv_copy(t, peer).wait_send()
        remote(cnt_s, cnt_r.at[me_g], ct_ss.at[t], ct_rs.at[t], (peer, me)).wait_send()
        return carry

    lax.fori_loop(1, groups, drain, 0)


def body(
    activations,
    slot_segment,
    attn_norm_gain,
    attn_norm_bias,
    mlp_norm_gain,
    mlp_norm_bias,
    qkv_weight,
    dense_weight,
    fc_weight,
    proj_weight,
):
    slots, width = activations.shape
    groups = lax.axis_size("req")
    members = lax.axis_size("mlp")
    model = qkv_weight.shape[0]
    rows = slots // 2
    half = rows // 2
    kv_w = dense_weight.shape[0]
    ff = fc_weight.shape[1]
    live_rows = slots // 2
    chips = members // 2
    dma = pltpu.SemaphoreType.DMA
    any_spec = pl.BlockSpec(memory_space=pl.ANY)
    vmem_spec = pl.BlockSpec(memory_space=pltpu.VMEM)
    vecs = [
        v.reshape(model // 128, 128)
        for v in (attn_norm_gain, attn_norm_bias, mlp_norm_gain, mlp_norm_bias)
    ]
    return pl.pallas_call(
        functools.partial(layer_kernel, groups, members),
        name="layer",
        out_shape=(
            jax.ShapeDtypeStruct((slots, width), F32),
            jax.ShapeDtypeStruct((2, live_rows, kv_w), BF16),
        ),
        in_specs=[any_spec] + [vmem_spec] * 5 + [any_spec] * 4,
        out_specs=(vmem_spec, vmem_spec),
        scratch_shapes=[
            pltpu.VMEM((2, members, rows, width), BF16),
            pltpu.VMEM(qkv_weight.shape, BF16),
            pltpu.VMEM(fc_weight.shape, BF16),
            pltpu.VMEM((kv_w + ff, model), BF16),
            pltpu.VMEM((rows, model), BF16),
            pltpu.VMEM((rows, model), BF16),
            pltpu.VMEM((4, members, width), F32),
            pltpu.VMEM((slots, 128), F32),
            pltpu.VMEM((3, slots, 128), F32),
            pltpu.VMEM((rows, kv_w), BF16),
            pltpu.VMEM((slots, 2 * kv_w), BF16),
            pltpu.VMEM((rows, kv_w + ff), BF16),
            pltpu.VMEM((slots, 2 * kv_w), BF16),
            pltpu.VMEM((slots, 2 * kv_w), BF16),
            pltpu.VMEM((8, 128), F32),
            pltpu.VMEM((groups, 8, 128), F32),
            pltpu.VMEM((2, chips, rows, width), BF16),
            pltpu.VMEM((2, chips, rows, width), BF16),
            pltpu.VMEM((2, chips, rows, width), F32),
            pltpu.VMEM((2, 2, half, width), BF16),
            pltpu.VMEM((2, 2, half, width), BF16),
            pltpu.VMEM((2, 2, 2, half, width), BF16),
            pltpu.VMEM((2, 2, 2, half, width), BF16),
            dma((4,)),
            dma((2,)),
            dma((2, 11)),
            dma((2, 11)),
            dma((groups,)),
            dma((groups,)),
            dma((groups,)),
            dma((groups,)),
            dma((2, chips)),
            dma((2, chips)),
            dma((2, 2)),
            dma((2, 2)),
            dma((2, 2, 2)),
            dma((2, 2, 2)),
        ],
        compiler_params=pltpu.CompilerParams(
            collective_id=0, has_side_effects=True, vmem_limit_bytes=62 * 1024 * 1024
        ),
    )(
        activations,
        slot_segment.reshape(slots // 128, 128),
        *vecs,
        qkv_weight,
        dense_weight,
        fc_weight,
        proj_weight,
    )


def solution(mesh):
    placed = (
        P("req", "mlp"),
        P("req"),
        P(),
        P(),
        P(),
        P(),
        P(None, "mlp"),
        P("mlp", None),
        P(None, "mlp"),
        P("mlp", None),
    )
    return jax.shard_map(
        body,
        mesh=mesh,
        in_specs=placed,
        out_specs=(P("req", "mlp"), P(None, "req", "mlp")),
        check_vma=False,
    )
```

time: 148 us -> 68.2 us (0.46)
  Pallas kernels: 0 us -> 62.7 us
  waiting for transfers between devices: 42.5 us -> 0 us
  matrix products: 41.2 us -> 0 us
  blocking collectives: 16.5 us -> 0 us
  between operations: 14.4 us -> 0.64 us
  local copies, waits for them, and re-layouts: 17.2 us -> 3.93 us
  other arithmetic: 12.3 us -> 0 us
  starting transfers between devices: 3.65 us -> 0 us
    pallas_call x0 -> x1, Pallas kernels: none -> 62.7 us  [body(): pl.pallas_call(functools.partial(layer_kernel, groups, members), name='la...]
    dot_general x4 -> x0, matrix products: 39.1 us -> none  [the longest x1 23.6 us: body(): jnp.dot(hidden, proj_weight, preferred_element_type=jnp.float32)]
    all_gather x1 -> x0, waiting for transfers between devices: 31.7 us -> none  [body(): full_rows = lax.all_gather(activations, 'mlp', axis=1, tiled=True)]
    unnamed x1 -> x0, blocking collectives: 16.5 us -> none
    all_to_all x1 -> x0, waiting for transfers between devices: 10.1 us -> none  [body(): lax.all_to_all(key_value, 'req', split_axis=1, concat_axis=0, tiled=True)]
    reduce_sum x3 -> x0, other arithmetic: 5.54 us -> none  [the longest x1 2.96 us: layer_norm(): row_mean = jnp.mean(row_data, axis=-1, keepdims=True)]
    all_to_all x1 -> x0, starting transfers between devices: 3.57 us -> none  [body(): lax.all_to_all(key_value, 'req', split_axis=1, concat_axis=0, tiled=True)]
    slice x4 -> x0, local copies, waits for them, and re-layouts: 2.66 us -> none  [the longest x2 1.71 us: rotate(): pass_part = head_data[..., ROT:]]
  transfers between devices with their start and end apart: 3 -> 0, of which waited for: 2 -> 0; matrix products, arithmetic and copies ran while one was open for 9% -> 0% of each run, Pallas kernels for 0% -> 0%
where the time goes in v1:
time: 68.2 us; the launch traced here: 67.2 us
  Pallas kernels  62.7 us (92%)
  local copies, waits for them, and re-layouts  3.93 us (6%)
    pallas_call x1, Pallas kernels, body(): pl.pallas_call(functools.partial(layer_kernel, groups, members), name='la...  62.7 us
    unnamed x2, local copies, waits for them, and re-layouts  3.93 us

profile of v1, /device:TPU:0, one launch (start us, length us, event | category | flops | bytes accessed | tf_op | source)
XLA Modules:
  0.0 67.2 jit_solution(8255290001086909982)
XLA Ops:
  0.6 62.7 %layer.1 = (f32[512,512]{1,0:T(8,128)}, bf16[2,256,256]{2,1,0:T(8,128)(2,1)}) custom-call(bf16[512,512]{1,0:T(8,128)(2,1)} %act.1, s32[4,128]{1,0:T(4,128)} %bitcast.9, f32[32,128]{1,0:T(8,128)} %bitcast.5, f32[32,128]{1,0:T(8,128)} %bitcast.6, f32[32,128]{1,0:T(8,128)} %bitcast.7, f32[32,128]{1,0:T(8,128)} %bitcast.8, bf16[4096,768]{1,0:T(8,128)(2,1)} %wq_h.1, ...), custom_call_target="tpu_custom_call" | custom-call | tf_op jit(solution)/shard_map/layer/pallas_call | solution.py:494
  63.3 2.3 %copy.14 = f32[512,512]{1,0:T(8,128)} copy(f32[512,512]{1,0:T(8,128)} %get-tuple-element.4) | data formatting | bytes 2097152
  65.6 1.7 %copy.15 = bf16[2,256,256]{2,1,0:T(8,128)(2,1)} copy(bf16[2,256,256]{2,1,0:T(8,128)(2,1)} %get-tuple-element.5) | data formatting | bytes 524288

commit v2 on v1

--- a/solution.py
+++ b/solution.py
@@ -16,6 +16,7 @@
 
 LA, LB, OA, RA, RB, OB, PP, PL, PR, POA, POB = range(11)
 OWN, RIGHT, OPP, LEFT = 0, 1, 2, 3
+PIECES = ((0, 128), (128, 256), (384, 128))
 
 
 def remote(src, dst, send_sem, recv_sem, dev):
@@ -67,6 +68,10 @@
     lo_r,
     lb_s,
     lb_r,
+    stat,
+    outv,
+    cachev,
+    osem,
     wsem,
     lsem,
     ag_ss,
@@ -82,9 +87,7 @@
     lb_ss,
     lb_rs,
 ):
-    rows = xf.shape[2]
-    half = rows // 2
-    width = xf.shape[3]
+    width = xf.shape[2]
     chips = members // 2
     model = members * width
     heads = qb.shape[1] // HD
@@ -108,8 +111,8 @@
         pltpu.make_async_copy(wp_h, wo.at[pl.ds(kv_w, wo.shape[0] - kv_w)], wsem.at[3]),
     ]
     own_copies = [
-        pltpu.make_async_copy(act.at[pl.ds(h * rows, rows)], xf.at[h, me], lsem.at[h])
-        for h in range(2)
+        pltpu.make_async_copy(act.at[pl.ds(base, rows)], xf.at[me, pl.ds(base, rows)], lsem.at[h])
+        for h, (base, rows) in enumerate(PIECES)
     ]
 
     barrier = pltpu.get_barrier_semaphore()
@@ -126,7 +129,17 @@
         c.start()
     pl.semaphore_wait(barrier, 3 + groups - 1)
 
-    lo_rows, hi_rows = pl.ds(0, half), pl.ds(half, half)
+    def span(h):
+        base, rows = PIECES[h]
+        return pl.ds(base, rows)
+
+    def upper(h):
+        base, rows = PIECES[h]
+        return pl.ds(base, rows // 2)
+
+    def lower(h):
+        base, rows = PIECES[h]
+        return pl.ds(base + rows // 2, rows // 2)
 
     def ag(h, kind, src, dst, dev):
         return remote(src, dst, ag_ss.at[h, kind], ag_rs.at[h, kind], dev)
@@ -141,39 +154,39 @@
         sent.append(copy)
 
     def gather_own(h):
-        a = act.at[pl.ds(h * rows, half)]
-        b = act.at[pl.ds(h * rows + half, half)]
-        go(ag(h, LA, a, xf.at[h, me, lo_rows], to_right))
-        go(ag(h, RB, b, xf.at[h, me, hi_rows], to_left))
-        go(ag(h, LB, b, xf.at[h, me, hi_rows], to_right))
-        go(ag(h, RA, a, xf.at[h, me, lo_rows], to_left))
-        go(ag(h, PP, act.at[pl.ds(h * rows, rows)], xf.at[h, me], to_partner))
+        a = act.at[upper(h)]
+        b = act.at[lower(h)]
+        go(ag(h, LA, a, xf.at[me, upper(h)], to_right))
+        go(ag(h, RB, b, xf.at[me, lower(h)], to_left))
+        go(ag(h, LB, b, xf.at[me, lower(h)], to_right))
+        go(ag(h, RA, a, xf.at[me, upper(h)], to_left))
+        go(ag(h, PP, act.at[span(h)], xf.at[me, span(h)], to_partner))
 
     def gather_far(h):
-        got(h, LA, xf.at[h, left, lo_rows])
-        go(ag(h, OA, xf.at[h, left, lo_rows], xf.at[h, left, lo_rows], to_right))
-        got(h, RB, xf.at[h, right, hi_rows])
-        go(ag(h, OB, xf.at[h, right, hi_rows], xf.at[h, right, hi_rows], to_left))
+        got(h, LA, xf.at[left, upper(h)])
+        go(ag(h, OA, xf.at[left, upper(h)], xf.at[left, upper(h)], to_right))
+        got(h, RB, xf.at[right, lower(h)])
+        go(ag(h, OB, xf.at[right, lower(h)], xf.at[right, lower(h)], to_left))
 
     def gather_near(h):
-        got(h, LB, xf.at[h, left, hi_rows])
-        go(ag(h, PL, xf.at[h, left], xf.at[h, left], to_partner))
-        got(h, RA, xf.at[h, right, lo_rows])
-        go(ag(h, PR, xf.at[h, right], xf.at[h, right], to_partner))
+        got(h, LB, xf.at[left, lower(h)])
+        go(ag(h, PL, xf.at[left, span(h)], xf.at[left, span(h)], to_partner))
+        got(h, RA, xf.at[right, upper(h)])
+        go(ag(h, PR, xf.at[right, span(h)], xf.at[right, span(h)], to_partner))
 
     def gather_opp(h):
-        got(h, OA, xf.at[h, opp, lo_rows])
-        go(ag(h, POA, xf.at[h, opp, lo_rows], xf.at[h, opp, lo_rows], to_partner))
-        got(h, OB, xf.at[h, opp, hi_rows])
-        go(ag(h, POB, xf.at[h, opp, hi_rows], xf.at[h, opp, hi_rows], to_partner))
+        got(h, OA, xf.at[opp, upper(h)])
+        go(ag(h, POA, xf.at[opp, upper(h)], xf.at[opp, upper(h)], to_partner))
+        got(h, OB, xf.at[opp, lower(h)])
+        go(ag(h, POB, xf.at[opp, lower(h)], xf.at[opp, lower(h)], to_partner))
 
     def gather_end(h):
         own_copies[h].wait()
-        got(h, PP, xf.at[h, partner])
-        got(h, PL, xf.at[h, left + flip])
-        got(h, PR, xf.at[h, right + flip])
-        got(h, POA, xf.at[h, opp + flip, lo_rows])
-        got(h, POB, xf.at[h, opp + flip, hi_rows])
+        got(h, PP, xf.at[partner, span(h)])
+        got(h, PL, xf.at[left + flip, span(h)])
+        got(h, PR, xf.at[right + flip, span(h)])
+        got(h, POA, xf.at[opp + flip, upper(h)])
+        got(h, POB, xf.at[opp + flip, lower(h)])
 
     gather_own(0)
 
@@ -217,28 +230,54 @@
     lax.fori_loop(1, groups, count_out, 0)
 
     def norms(h):
-        def body(r, carry):
-            at = pl.ds(pl.multiple_of(r * 16, 16), 16)
-            xs = [xf[h, m, at, :].astype(F32) for m in range(members)]
-            total = functools.reduce(lambda a, b: a + b, xs)
-            mean = jnp.sum(total, axis=-1, keepdims=True) * (1.0 / model)
-            cs = [x - mean for x in xs]
-            square = functools.reduce(lambda a, b: a + b, [c * c for c in cs])
-            scale = lax.rsqrt(jnp.sum(square, axis=-1, keepdims=True) * (1.0 / model) + 1e-05)
-            for m in range(members):
-                y = cs[m] * scale
-                cols = slice(m * width, (m + 1) * width)
-                n1[at, cols] = (y * gs[0, m : m + 1, :] + gs[1, m : m + 1, :]).astype(BF16)
-                n2[at, cols] = (y * gs[2, m : m + 1, :] + gs[3, m : m + 1, :]).astype(BF16)
+        base, rows = PIECES[h]
+        tiles = [(m, slice(k * 128, (k + 1) * 128)) for m in range(members) for k in range(width // 128)]
+
+        def sums(r, carry):
+            to = pl.ds(pl.multiple_of(r * 16, 16), 16)
+            at = pl.ds(pl.multiple_of(base + r * 16, 16), 16)
+            parts = [jnp.zeros((16, 128), F32)] * 4
+            for n, (m, cols) in enumerate(tiles):
+                parts[n % 4] = parts[n % 4] + xf[m, at, cols].astype(F32)
+            stat[2, to, :] = (parts[0] + parts[1]) + (parts[2] + parts[3])
             return carry
 
-        lax.fori_loop(0, rows // 16, body, 0)
+        def squares(r, carry):
+            to = pl.ds(pl.multiple_of(r * 16, 16), 16)
+            at = pl.ds(pl.multiple_of(base + r * 16, 16), 16)
+            mean = stat[0, to, :]
+            parts = [jnp.zeros((16, 128), F32)] * 4
+            for n, (m, cols) in enumerate(tiles):
+                c = xf[m, at, cols].astype(F32) - mean
+                parts[n % 4] = parts[n % 4] + c * c
+            stat[2, to, :] = (parts[0] + parts[1]) + (parts[2] + parts[3])
+            return carry
+
+        def apply(r, carry):
+            to = pl.ds(pl.multiple_of(r * 32, 32), 32)
+            at = pl.ds(pl.multiple_of(base + r * 32, 32), 32)
+            mean, scale = stat[0, to, :], stat[1, to, :]
+            for m, cols in tiles:
+                y = (xf[m, at, cols].astype(F32) - mean) * scale
+                k = slice(m * width + cols.start, m * width + cols.stop)
+                n1[to, k] = (y * gs[0, m : m + 1, cols] + gs[1, m : m + 1, cols]).astype(BF16)
+                n2[to, k] = (y * gs[2, m : m + 1, cols] + gs[3, m : m + 1, cols]).astype(BF16)
+            return carry
+
+        lax.fori_loop(0, rows // 16, sums, 0)
+        mean = jnp.sum(stat[2, 0:rows, :], axis=-1, keepdims=True) * (1.0 / model)
+        stat[0, 0:rows, :] = jnp.broadcast_to(mean, (rows, 128))
+        lax.fori_loop(0, rows // 16, squares, 0)
+        var = jnp.sum(stat[2, 0:rows, :], axis=-1, keepdims=True) * (1.0 / model)
+        stat[1, 0:rows, :] = jnp.broadcast_to(lax.rsqrt(var + 1e-05), (rows, 128))
+        lax.fori_loop(0, rows // 32, apply, 0)
 
     def project(h):
-        at = slice(h * rows, (h + 1) * rows)
+        base, rows = PIECES[h]
+        at = slice(base, base + rows)
         parts = []
         for n in range(wq.shape[1] // 256):
-            acc = jnp.dot(n1[...], wq[:, n * 256 : (n + 1) * 256], preferred_element_type=F32)
+            acc = jnp.dot(n1[0:rows, :], wq[:, n * 256 : (n + 1) * 256], preferred_element_type=F32)
             parts += [acc[:, :HD], acc[:, HD:]]
         cos, s1, s2 = tab[0, at, :], tab[1, at, :], tab[2, at, :]
 
@@ -247,20 +286,21 @@
 
         for i in range(heads):
             cols = slice(i * HD, (i + 1) * HD)
-            qb[:, cols] = turn(parts[3 * i]).astype(BF16)
+            qb[0:rows, cols] = turn(parts[3 * i]).astype(BF16)
             kvb[at, cols] = turn(parts[3 * i + 1]).astype(BF16)
             kvb[at, kv_w + i * HD : kv_w + (i + 1) * HD] = parts[3 * i + 2].astype(BF16)
 
     def attend(h):
-        keys = (h + 1) * rows
-        first = jnp.concatenate([segc[h * rows : (h + 1) * rows, :]] * (keys // 128), axis=1)
-        query = (h * rows + lax.broadcasted_iota(jnp.int32, (rows, keys), 0)).astype(F32)
+        base, rows = PIECES[h]
+        keys = base + rows
+        first = jnp.concatenate([segc[base : base + rows, :]] * (keys // 128), axis=1)
+        query = (base + lax.broadcasted_iota(jnp.int32, (rows, keys), 0)).astype(F32)
         key = lax.broadcasted_iota(jnp.int32, (rows, keys), 1).astype(F32)
         allowed = (key >= first) & (key <= query)
         for i in range(heads):
             cols = slice(i * HD, (i + 1) * HD)
             s = lax.dot_general(
-                qb[:, cols],
+                qb[0:rows, cols],
                 kvb[0:keys, cols],
                 (((1,), (1,)), ((), ())),
                 preferred_element_type=F32,
@@ -271,64 +311,74 @@
             ctx = jnp.dot(
                 p, kvb[0:keys, kv_w + i * HD : kv_w + (i + 1) * HD], preferred_element_type=F32
             )
-            hc[:, cols] = ctx.astype(BF16)
+            hc[0:rows, cols] = ctx.astype(BF16)
 
     def expand(h):
+        rows = PIECES[h][1]
         for n in range(wf.shape[1] // 256):
             cols = slice(n * 256, (n + 1) * 256)
-            u = jnp.dot(n2[...], wf[:, cols], preferred_element_type=F32)
+            u = jnp.dot(n2[0:rows, :], wf[:, cols], preferred_element_type=F32)
             u = 0.5 * u * (1.0 + lax.erf(u * (0.5**0.5)))
-            hc[:, kv_w + n * 256 : kv_w + (n + 1) * 256] = u.astype(BF16)
+            hc[0:rows, kv_w + n * 256 : kv_w + (n + 1) * 256] = u.astype(BF16)
 
     def pcopy(h, rel):
-        return remote(psend.at[h, rel], precv.at[h, rel], p_ss.at[h, rel], p_rs.at[h, rel], to_partner)
+        return remote(psend.at[rel, span(h)], precv.at[rel, span(h)], p_ss.at[h, rel], p_rs.at[h, rel], to_partner)
 
     def contract(h, rel):
+        base, rows = PIECES[h]
         block = 2 * lax.rem(chip + rel, chips)
         for theirs in (True, False):
             col = (block + (1 - core if theirs else core)) * width
             acc = jnp.dot(
-                hc[...],
+                hc[0:rows, :],
                 wo[:, pl.ds(pl.multiple_of(col, width), width)],
                 preferred_element_type=F32,
             )
             if theirs:
-                psend[h, rel] = acc.astype(BF16)
+                psend[rel, base : base + rows, :] = acc.astype(BF16)
                 go(pcopy(h, rel))
             else:
-                mine[h, rel] = acc
-
-    def chip_sum(h, rel, at=slice(None)):
-        return mine[h, rel, at, :] + precv[h, rel, at, :].astype(F32)
+                mine[rel, base : base + rows, :] = acc
+
+    def side(h, piece):
+        base, rows = PIECES[h]
+        half = rows // 2
+        return slice(base + piece * half, base + (piece + 1) * half)
+
+    def fold(h):
+        base, rows = PIECES[h]
+        return pl.ds(base // 2, rows // 2)
+
+    def chip_sum(h, rel, piece):
+        at = side(h, piece)
+        return mine[rel, at, :] + precv[rel, at, :].astype(F32)
 
     def low(h, way):
         dev = to_right if way == 0 else to_left
-        return remote(lo_s.at[h, way], lo_r.at[h, way], lo_ss.at[h, way], lo_rs.at[h, way], dev)
+        return remote(lo_s.at[way, fold(h)], lo_r.at[way, fold(h)], lo_ss.at[h, way], lo_rs.at[h, way], dev)
 
     def back(h, way, piece):
         dev = to_right if way == 0 else to_left
         return remote(
-            lb_s.at[h, way, piece],
-            lb_r.at[h, way, piece],
+            lb_s.at[way, piece, fold(h)],
+            lb_r.at[way, piece, fold(h)],
             lb_ss.at[h, way, piece],
             lb_rs.at[h, way, piece],
             dev,
         )
 
-    top, bottom = slice(0, half), slice(half, rows)
-
     def scatter_opp(h):
         pcopy(h, OPP).wait_recv()
-        lo_s[h, 0] = chip_sum(h, OPP, top).astype(BF16)
+        lo_s[0, fold(h)] = chip_sum(h, OPP, 0).astype(BF16)
         go(low(h, 0))
-        lo_s[h, 1] = chip_sum(h, OPP, bottom).astype(BF16)
+        lo_s[1, fold(h)] = chip_sum(h, OPP, 1).astype(BF16)
         go(low(h, 1))
 
     def scatter_near(h, way):
         rel = RIGHT if way == 0 else LEFT
         piece = 1 - way
         pcopy(h, rel).wait_recv()
-        lb_s[h, way, piece] = chip_sum(h, rel, (top, bottom)[piece]).astype(BF16)
+        lb_s[way, piece, fold(h)] = chip_sum(h, rel, piece).astype(BF16)
         go(back(h, way, piece))
 
     def scatter_far(h):
@@ -336,8 +386,8 @@
             rel = RIGHT if way == 0 else LEFT
             piece = way
             low(h, way).wait_recv()
-            total = chip_sum(h, rel, (top, bottom)[piece]) + lo_r[h, way].astype(F32)
-            lb_s[h, way, piece] = total.astype(BF16)
+            total = chip_sum(h, rel, piece) + lo_r[way, fold(h)].astype(F32)
+            lb_s[way, piece, fold(h)] = total.astype(BF16)
             go(back(h, way, piece))
 
     def finish(h):
@@ -345,13 +395,16 @@
         for piece in range(2):
             for way in range(2):
                 back(h, way, piece).wait_recv()
-            at = (top, bottom)[piece]
-            total = chip_sum(h, OWN, at)
-            total = total + lb_r[h, 0, piece].astype(F32) + lb_r[h, 1, piece].astype(F32)
-            base = h * rows + piece * half
-            x = xf[h, me, at, :].astype(F32)
-            first = jnp.concatenate([segc[base : base + half, :]] * (width // 128), axis=1)
-            out[base : base + half, :] = jnp.where(first >= 0.0, x + total, 0.0)
+            at = side(h, piece)
+            total = chip_sum(h, OWN, piece)
+            total = total + lb_r[0, piece, fold(h)].astype(F32) + lb_r[1, piece, fold(h)].astype(F32)
+            x = xf[me, at, :].astype(F32)
+            first = jnp.concatenate([segc[at, :]] * (width // 128), axis=1)
+            outv[at, :] = jnp.where(first >= 0.0, x + total, 0.0)
+        out_copy(h).start()
+
+    def out_copy(h):
+        return pltpu.make_async_copy(outv.at[span(h)], out.at[span(h)], osem.at[h])
 
     def cache_out():
         slots = kvp.shape[0]
@@ -409,14 +462,18 @@
             acc = acc + jnp.dot(
                 pick, kvr[b * 128 : (b + 1) * 128, :], preferred_element_type=F32
             )
-        cache[0] = acc[:, :kv_w].astype(BF16)
-        cache[1] = acc[:, kv_w:].astype(BF16)
+        cachev[0] = acc[:, :kv_w].astype(BF16)
+        cachev[1] = acc[:, kv_w:].astype(BF16)
+        cache_copy.start()
+
+    cache_copy = pltpu.make_async_copy(cachev, cache, osem.at[len(PIECES)])
 
     gather_end(0)
     norms(0)
     copies[0].wait()
     project(0)
     gather_far(1)
+    gather_own(2)
     attend(0)
     copies[1].wait()
     expand(0)
@@ -425,17 +482,19 @@
     copies[3].wait()
     contract(0, OPP)
     contract(0, RIGHT)
-    gather_opp(1)
     scatter_opp(0)
     contract(0, LEFT)
+    gather_opp(1)
     scatter_near(0, 0)
     contract(0, OWN)
     scatter_near(0, 1)
+    gather_far(2)
     gather_end(1)
     norms(1)
+    gather_near(2)
     scatter_far(0)
     project(1)
-    cache_out()
+    gather_opp(2)
     attend(1)
     expand(1)
     contract(1, OPP)
@@ -445,10 +504,25 @@
     scatter_near(1, 0)
     contract(1, OWN)
     scatter_near(1, 1)
+    gather_end(2)
+    norms(2)
+    project(2)
+    cache_out()
+    attend(2)
+    scatter_far(1)
+    expand(2)
+    contract(2, OPP)
+    contract(2, RIGHT)
+    scatter_opp(2)
+    contract(2, LEFT)
+    scatter_near(2, 0)
+    contract(2, OWN)
+    scatter_near(2, 1)
     finish(0)
+    scatter_far(2)
     cache_in()
-    scatter_far(1)
     finish(1)
+    finish(2)
 
     for copy in sent:
         copy.wait_send()
@@ -460,6 +534,9 @@
         return carry
 
     lax.fori_loop(1, groups, drain, 0)
+    cache_copy.wait()
+    for h in range(len(PIECES)):
+        out_copy(h).wait()
 
 
 def body(
@@ -478,8 +555,9 @@
     groups = lax.axis_size("req")
     members = lax.axis_size("mlp")
     model = qkv_weight.shape[0]
-    rows = slots // 2
-    half = rows // 2
+    pieces = len(PIECES)
+    rows = max(size for _, size in PIECES)
+    half = slots // 2
     kv_w = dense_weight.shape[0]
     ff = fc_weight.shape[1]
     live_rows = slots // 2
@@ -499,9 +577,9 @@
             jax.ShapeDtypeStruct((2, live_rows, kv_w), BF16),
         ),
         in_specs=[any_spec] + [vmem_spec] * 5 + [any_spec] * 4,
-        out_specs=(vmem_spec, vmem_spec),
+        out_specs=(any_spec, any_spec),
         scratch_shapes=[
-            pltpu.VMEM((2, members, rows, width), BF16),
+            pltpu.VMEM((members, slots, width), BF16),
             pltpu.VMEM(qkv_weight.shape, BF16),
             pltpu.VMEM(fc_weight.shape, BF16),
             pltpu.VMEM((kv_w + ff, model), BF16),
@@ -517,27 +595,31 @@
             pltpu.VMEM((slots, 2 * kv_w), BF16),
             pltpu.VMEM((8, 128), F32),
             pltpu.VMEM((groups, 8, 128), F32),
-            pltpu.VMEM((2, chips, rows, width), BF16),
-            pltpu.VMEM((2, chips, rows, width), BF16),
-            pltpu.VMEM((2, chips, rows, width), F32),
+            pltpu.VMEM((chips, slots, width), BF16),
+            pltpu.VMEM((chips, slots, width), BF16),
+            pltpu.VMEM((chips, slots, width), F32),
+            pltpu.VMEM((2, half, width), BF16),
+            pltpu.VMEM((2, half, width), BF16),
             pltpu.VMEM((2, 2, half, width), BF16),
             pltpu.VMEM((2, 2, half, width), BF16),
-            pltpu.VMEM((2, 2, 2, half, width), BF16),
-            pltpu.VMEM((2, 2, 2, half, width), BF16),
+            pltpu.VMEM((3, rows, 128), F32),
+            pltpu.VMEM((slots, width), F32),
+            pltpu.VMEM((2, live_rows, kv_w), BF16),
+            dma((pieces + 1,)),
             dma((4,)),
-            dma((2,)),
-            dma((2, 11)),
-            dma((2, 11)),
+            dma((pieces,)),
+            dma((pieces, 11)),
+            dma((pieces, 11)),
             dma((groups,)),
             dma((groups,)),
             dma((groups,)),
             dma((groups,)),
-            dma((2, chips)),
-            dma((2, chips)),
-            dma((2, 2)),
-            dma((2, 2)),
-            dma((2, 2, 2)),
-            dma((2, 2, 2)),
+            dma((pieces, chips)),
+            dma((pieces, chips)),
+            dma((pieces, 2)),
+            dma((pieces, 2)),
+            dma((pieces, 2, 2)),
+            dma((pieces, 2, 2)),
         ],
         compiler_params=pltpu.CompilerParams(
             collective_id=0, has_side_effects=True, vmem_limit_bytes=62 * 1024 * 1024

time: 68.2 us -> 62.8 us (0.921)
  Pallas kernels: 62.7 us -> 57.9 us
    pallas_call x1, Pallas kernels: 62.7 us -> 57.9 us  [body(): pl.pallas_call(functools.partial(layer_kernel, groups, members), name='la...]
where the time goes in v2:
time: 62.8 us; the launch traced here: 62.5 us
  Pallas kernels  57.9 us (92%)
  local copies, waits for them, and re-layouts  3.93 us (6%)
  between operations  0.64 us (1%)
    pallas_call x1, Pallas kernels, body(): pl.pallas_call(functools.partial(layer_kernel, groups, members), name='la...  57.9 us
    unnamed x2, local copies, waits for them, and re-layouts  3.93 us

profile of v2, /device:TPU:0, one launch (start us, length us, event | category | flops | bytes accessed | tf_op | source)
XLA Modules:
  0.0 62.5 jit_solution(18391772633683309147)
XLA Ops:
  0.6 57.9 %layer.1 = (f32[512,512]{1,0:T(8,128)}, bf16[2,256,256]{2,1,0:T(8,128)(2,1)}) custom-call(bf16[512,512]{1,0:T(8,128)(2,1)} %act.1, s32[4,128]{1,0:T(4,128)} %bitcast.9, f32[32,128]{1,0:T(8,128)} %bitcast.5, f32[32,128]{1,0:T(8,128)} %bitcast.6, f32[32,128]{1,0:T(8,128)} %bitcast.7, f32[32,128]{1,0:T(8,128)} %bitcast.8, bf16[4096,768]{1,0:T(8,128)(2,1)} %wq_h.1, ...), custom_call_target="tpu_custom_call" | custom-call | tf_op jit(solution)/shard_map/layer/pallas_call | solution.py:572
  58.6 2.3 %copy.14 = f32[512,512]{1,0:T(8,128)} copy(f32[512,512]{1,0:T(8,128)} %get-tuple-element.4) | data formatting | bytes 2097152
  60.8 1.7 %copy.15 = bf16[2,256,256]{2,1,0:T(8,128)(2,1)} copy(bf16[2,256,256]{2,1,0:T(8,128)(2,1)} %get-tuple-element.5) | data formatting | bytes 524288

commit v3 on v2

--- a/solution.py
+++ b/solution.py
@@ -218,8 +218,9 @@
 
     gather_far(0)
     gather_own(1)
-    lax.fori_loop(0, seg.shape[0], angles, 0)
+    lax.fori_loop(0, seg.shape[0] // 2, angles, 0)
     gather_near(0)
+    lax.fori_loop(seg.shape[0] // 2, seg.shape[0], angles, 0)
     gather_opp(0)
 
     def count_out(t, carry):
@@ -539,6 +540,44 @@
         out_copy(h).wait()
 
 
+def deliver_kernel(rows_h, cache_h, rows_o, cache_o, rows_v, cache_v, isem, osem):
+    step = rows_h.shape[0] // 4
+    parts = [
+        (rows_h.at[s], rows_v.at[s], rows_o.at[s])
+        for s in (pl.ds(i * step, step) for i in range(4))
+    ]
+    parts.insert(0, (cache_h, cache_v, cache_o))
+    inward = [pltpu.make_async_copy(a, v, isem.at[i]) for i, (a, v, _) in enumerate(parts)]
+    outward = [pltpu.make_async_copy(v, o, osem.at[i]) for i, (_, v, o) in enumerate(parts)]
+    for c in inward:
+        c.start()
+    for i, o in zip(inward, outward):
+        i.wait()
+        o.start()
+    for o in outward:
+        o.wait()
+
+
+def deliver(rows, cache):
+    any_spec = pl.BlockSpec(memory_space=pl.ANY)
+    return pl.pallas_call(
+        deliver_kernel,
+        name="deliver",
+        out_shape=(
+            jax.ShapeDtypeStruct(rows.shape, rows.dtype),
+            jax.ShapeDtypeStruct(cache.shape, cache.dtype),
+        ),
+        in_specs=[any_spec] * 2,
+        out_specs=(any_spec, any_spec),
+        scratch_shapes=[
+            pltpu.VMEM(rows.shape, rows.dtype),
+            pltpu.VMEM(cache.shape, cache.dtype),
+            pltpu.SemaphoreType.DMA((5,)),
+            pltpu.SemaphoreType.DMA((5,)),
+        ],
+    )(rows, cache)
+
+
 def body(
     activations,
     slot_segment,
@@ -569,7 +608,7 @@
         v.reshape(model // 128, 128)
         for v in (attn_norm_gain, attn_norm_bias, mlp_norm_gain, mlp_norm_bias)
     ]
-    return pl.pallas_call(
+    results = pl.pallas_call(
         functools.partial(layer_kernel, groups, members),
         name="layer",
         out_shape=(
@@ -633,6 +672,7 @@
         fc_weight,
         proj_weight,
     )
+    return deliver(*results)
 
 
 def solution(mesh):

time: 62.8 us -> 61.1 us (0.973)
  local copies, waits for them, and re-layouts: 3.93 us -> 0 us
  Pallas kernels: 57.9 us -> 60 us
    unnamed x2 -> x0, local copies, waits for them, and re-layouts: 3.93 us -> none
    pallas_call x0 -> x1, Pallas kernels: none -> 2.08 us  [deliver(): pl.pallas_call(deliver_kernel, name='deliver', out_shape=(jax.ShapeDtypeS...]
where the time goes in v3:
time: 61.1 us; the launch traced here: 60.8 us
  Pallas kernels  60 us (98%)
  between operations  0.82 us (1%)
    pallas_call x1, Pallas kernels, body(): pl.pallas_call(functools.partial(layer_kernel, groups, members), name='la...  57.9 us
    pallas_call x1, Pallas kernels, deliver(): pl.pallas_call(deliver_kernel, name='deliver', out_shape=(jax.ShapeDtypeS...  2.08 us

profile of v3, /device:TPU:0, one launch (start us, length us, event | category | flops | bytes accessed | tf_op | source)
XLA Modules:
  0.0 60.8 jit_solution(136768502745702905)
XLA Ops:
  0.6 57.9 %layer.1 = (f32[512,512]{1,0:T(8,128)}, bf16[2,256,256]{2,1,0:T(8,128)(2,1)}) custom-call(bf16[512,512]{1,0:T(8,128)(2,1)} %act.1, s32[4,128]{1,0:T(4,128)} %bitcast.9, f32[32,128]{1,0:T(8,128)} %bitcast.5, f32[32,128]{1,0:T(8,128)} %bitcast.6, f32[32,128]{1,0:T(8,128)} %bitcast.7, f32[32,128]{1,0:T(8,128)} %bitcast.8, bf16[4096,768]{1,0:T(8,128)(2,1)} %wq_h.1, ...), custom_call_target="tpu_custom_call" | custom-call | tf_op jit(solution)/shard_map/layer/pallas_call | solution.py:611
  58.6 2.1 %deliver.1 = (f32[512,512]{1,0:T(8,128)}, bf16[2,256,256]{2,1,0:T(8,128)(2,1)}) custom-call(f32[512,512]{1,0:T(8,128)} %get-tuple-element.4.rows_h, bf16[2,256,256]{2,1,0:T(8,128)(2,1)} %get-tuple-element.5.cache_h), custom_call_target="tpu_custom_call" | custom-call | tf_op jit(solution)/shard_map/deliver/pallas_call | solution.py:563
